TPU v7x, 32 devices: a whole 2x2x4 slice. The times are simulated.
32 devices in a mesh: scen: 8 (over y, x, core), veh: 4 (over z).
Axes of the slice: x: 2, y: 2, z: 4, core: 2. Of those that a mesh axis runs over, the one named last changes fastest.
Arguments:
- start_plan: bfloat16 [128, 3584, 128], P('scen', 'veh'), may hold values from -6 to 6
- linear_cost: bfloat16 [128, 3584, 128], P('scen', 'veh'), may hold values from -12 to 12
- price: bfloat16 [128, 3584, 128], P('scen', 'veh'), may hold values from -6 to 6
- anchor: bfloat16 [8, 3584, 128], P(None, 'veh'), may hold values from -6 to 6
- hessian: bfloat16 [128, 128, 128], P('scen'), as said below
- usage_coef: bfloat16 [3584, 128], P('veh'), may hold values from -1.5 to 1.5
- crew_limit: float32 [128, 350], P('scen'), may hold values from -48 to 48
- crew_dual: float32 [128, 350], P('scen'), may hold values from 0 to 2
- crew_row: int32 [3584], P('veh'), may hold values from 0 to 349
- bundle_of: int32 [128, 1], replicated, may hold values from 0 to 7
- scen_weight: int32 [128], replicated, may hold values from 1 to 8
Outputs:
- new_plan: bfloat16 [128, 3584, 128], P('scen', 'veh')
- new_price: bfloat16 [128, 3584, 128], P('scen', 'veh')
- bundle_mean: bfloat16 [8, 3584, 128], P('scen', 'veh')
- new_dual: float32 [128, 350], P('scen')
- gap: float32 [], replicated
Inputs may be any that keep to these rules, and one draw needn't show every extreme that they name: `bundle_of`: every bundle holds one scenario or more. `hessian`: symmetric.
All inputs are finite; a program needn't handle non-finite values.
Results may differ from a plain program's by a relative error of at most 0.0013.
The roundings to bfloat16 on the way count: a program that leaves them out, or rounds other values in their place, can miss the bound.
Values sent between devices are 32-bit elements; how exact they have to be, the bound alone decides.
A program may use at most 128 MiB of HBM per device.

v0:
```python
import jax
import jax.numpy as jnp
from jax import lax
from jax.sharding import PartitionSpec as P

ITERS = 12


penalty = 1.0
step_size = 0.02
dual_step = 0.02
highest = lax.Precision.HIGHEST


def shards(
    start_plan,
    linear_cost,
    price,
    anchor,
    hessian,
    usage_coef,
    crew_limit,
    crew_dual,
    crew_row,
    bundle_of,
    scen_weight,
):
    local_scen = start_plan.shape[0]
    bundle_count = anchor.shape[0]
    crew_count = crew_limit.shape[1]
    offset = lax.axis_index("scen") * local_scen
    all_bundles = bundle_of[:, 0]
    my_bundles = lax.dynamic_slice_in_dim(all_bundles, offset, local_scen)
    my_weights = lax.dynamic_slice_in_dim(scen_weight, offset, local_scen).astype(jnp.float32)
    bundle_ids = jnp.arange(bundle_count, dtype=jnp.int32)
    selector = (my_bundles[:, None] == bundle_ids[None, :]).astype(jnp.float32)
    anchored = jnp.einsum(
        "sb,bvi->svi", selector.astype(jnp.bfloat16), anchor, preferred_element_type=jnp.float32
    )
    linear_part = linear_cost.astype(jnp.float32) + price.astype(jnp.float32) - penalty * anchored
    coefficient = usage_coef.astype(jnp.float32)
    crew_map = (crew_row[:, None] == jnp.arange(crew_count, dtype=jnp.int32)[None, :]).astype(
        jnp.float32
    )

    def advance(index, state_pair):
        roster, multiplier = state_pair
        rounded = roster.astype(jnp.bfloat16)
        curvature = jnp.einsum("svi,sij->svj", rounded, hessian, preferred_element_type=jnp.float32)
        consumed = jnp.sum(roster * coefficient[None], axis=2)
        partial_use = jnp.dot(consumed, crew_map, precision=highest)
        usage = lax.psum(partial_use, "veh")
        updated = jnp.maximum(multiplier + dual_step * (usage - crew_limit), 0.0)
        per_vehicle = jnp.dot(multiplier, crew_map.T, precision=highest)
        gradient = (
            curvature + linear_part + penalty * roster + per_vehicle[:, :, None] * coefficient[None]
        )
        return (roster - step_size * gradient, updated)

    roster, multiplier = lax.fori_loop(
        0, ITERS, advance, (start_plan.astype(jnp.float32), crew_dual)
    )
    weighted_pick = selector * my_weights[:, None]
    every_weight = jnp.sum(
        (all_bundles[:, None] == bundle_ids[None, :]).astype(jnp.float32)
        * scen_weight.astype(jnp.float32)[:, None],
        axis=0,
    )
    owned_rows = bundle_count // lax.axis_size("scen")
    own_start = lax.axis_index("scen") * owned_rows
    partial_sums = jnp.einsum("sb,svi->bvi", weighted_pick, roster, precision=highest)
    totals = lax.psum(partial_sums, "scen")
    every_mean = totals / every_weight[:, None, None]
    own_mean = lax.dynamic_slice_in_dim(every_mean, own_start, owned_rows)
    mean_here = jnp.einsum("sb,bvi->svi", selector, every_mean, precision=highest)
    deviation = roster - mean_here
    new_price = (price.astype(jnp.float32) + penalty * deviation).astype(jnp.bfloat16)
    spread = jnp.sum(my_weights * jnp.sum(deviation * deviation, axis=(1, 2)))
    spread_total = lax.psum(spread, ("scen", "veh"))
    entries = start_plan.shape[1] * lax.axis_size("veh") * start_plan.shape[2]
    gap = jnp.sqrt(spread_total / (jnp.sum(scen_weight.astype(jnp.float32)) * entries))
    return (roster.astype(jnp.bfloat16), new_price, own_mean.astype(jnp.bfloat16), multiplier, gap)


def solution(mesh):
    return jax.shard_map(
        shards,
        mesh=mesh,
        in_specs=(
            P("scen", "veh", None),
            P("scen", "veh", None),
            P("scen", "veh", None),
            P(None, "veh", None),
            P("scen", None, None),
            P("veh", None),
            P("scen", None),
            P("scen", None),
            P("veh"),
            P(),
            P(),
        ),
        out_specs=(
            P("scen", "veh", None),
            P("scen", "veh", None),
            P("scen", "veh", None),
            P("scen", None),
            P(),
        ),
        check_vma=False,
    )
```

profile of v0, /device:TPU:0, one launch (start us, length us, event | category | flops | bytes accessed | tf_op | source)
XLA Modules:
  0.0 568.2 jit_solution(2180171724463665782)
XLA Ops:
  8.7 22.6 %fusion.12 = f32[16,896,128]{2,0,1:T(8,128)S(1)} fusion(bf16[16,896,128]{2,1,0:T(8,128)(2,1)} %param.14, bf16[16,896,128]{2,1,0:T(8,128)(2,1)} %param.15, bf16[8,896,128]{2,1,0:T(8,128)(2,1)S(1)} %copy-done, s32[16]{0:T(128)S(1)} %dynamic-slice_bitcast_fusion), kind=kOutput, calls=%fused_computation.15 | convolution fusion | flops 36700544 | bytes 16515136 | tf_op jit(solution)/shard_map/sb,bvi->svi/dot_general | solution.py:37
  31.3 5.2 copy.27
  36.5 3.8 convert_element_type.42
  40.4 364.3 %while.13 = (s32[]{:T(128)}, f32[16,896,128]{2,1,0:T(8,128)}, f32[16,350]{1,0:T(8,128)S(1)}, bf16[16,128,128]{2,1,0:T(8,128)(2,1)S(1)}, f32[16,896,128]{2,1,0:T(...) while((s32[]{:T(128)}, f32[16,896,128]{2,1,0:T(8,128)}, ...), condition=%wide.region_3.0_spmd.clone, body=%wide.region_0.0_spmd.clone.sunk | while | flops 607967616 | bytes 75257976 | solution.py:60
  40.4 3.1 copy.53
  47.0 5.9 %multiply_subtract_fusion.2 = f32[16,896,128]{2,1,0:T(8,128)} fusion(f32[16,896,128]{2,1,0:T(8,128)S(1)} %copy.53, f32[16,896,128]{2,1,0:T(8,128)S(1)} %copy-done.1, f32[896,128]{1,0:T(8,128)S(1)} %get-tuple-element.185, f32[16,896]{1,0:T(8,128)S(1)} %fusion.47, bf16[16,128,128]{2,1,0:T(8,128)(2,1)S(1)} %get-tuple-element.183), kind=kOutput, calls=%fused_computation.2.clone.1 | convolution fusion | flops 482607104 | bytes 23060480 | tf_op jit(solution)/shard_map/while/body/eval_jaxpr/svi,sij->svj/dot_general | solution.py:49
  53.8 20.8 %psum.25 = f32[16,350]{1,0:T(8,128)S(1)} all-reduce(f32[16,350]{1,0:T(8,128)S(1)} %fusion.48), channel_id=1, replica_groups=mesh['scen'=8,'veh'=4] {'veh'}, use_global_device_ids=true, to_apply=%region_2.0 | all-reduce | flops 5600 | bytes 44800 | tf_op jit(solution)/shard_map/while/body/eval_jaxpr/psum | solution.py:52
  74.6 3.1 copy.53
  81.1 5.9 %multiply_subtract_fusion.2 = f32[16,896,128]{2,1,0:T(8,128)} fusion(f32[16,896,128]{2,1,0:T(8,128)S(1)} %copy.53, f32[16,896,128]{2,1,0:T(8,128)S(1)} %copy-done.1, f32[896,128]{1,0:T(8,128)S(1)} %get-tuple-element.185, f32[16,896]{1,0:T(8,128)S(1)} %fusion.47, bf16[16,128,128]{2,1,0:T(8,128)(2,1)S(1)} %get-tuple-element.183), kind=kOutput, calls=%fused_computation.2.clone.1 | convolution fusion | flops 482607104 | bytes 23060480 | tf_op jit(solution)/shard_map/while/body/eval_jaxpr/svi,sij->svj/dot_general | solution.py:49
  88.0 15.8 %psum.25 = f32[16,350]{1,0:T(8,128)S(1)} all-reduce(f32[16,350]{1,0:T(8,128)S(1)} %fusion.48), channel_id=1, replica_groups=mesh['scen'=8,'veh'=4] {'veh'}, use_global_device_ids=true, to_apply=%region_2.0 | all-reduce | flops 5600 | bytes 44800 | tf_op jit(solution)/shard_map/while/body/eval_jaxpr/psum | solution.py:52
  103.8 3.1 copy.53
  110.4 5.9 %multiply_subtract_fusion.2 = f32[16,896,128]{2,1,0:T(8,128)} fusion(f32[16,896,128]{2,1,0:T(8,128)S(1)} %copy.53, f32[16,896,128]{2,1,0:T(8,128)S(1)} %copy-done.1, f32[896,128]{1,0:T(8,128)S(1)} %get-tuple-element.185, f32[16,896]{1,0:T(8,128)S(1)} %fusion.47, bf16[16,128,128]{2,1,0:T(8,128)(2,1)S(1)} %get-tuple-element.183), kind=kOutput, calls=%fused_computation.2.clone.1 | convolution fusion | flops 482607104 | bytes 23060480 | tf_op jit(solution)/shard_map/while/body/eval_jaxpr/svi,sij->svj/dot_general | solution.py:49
  117.2 17.4 %psum.25 = f32[16,350]{1,0:T(8,128)S(1)} all-reduce(f32[16,350]{1,0:T(8,128)S(1)} %fusion.48), channel_id=1, replica_groups=mesh['scen'=8,'veh'=4] {'veh'}, use_global_device_ids=true, to_apply=%region_2.0 | all-reduce | flops 5600 | bytes 44800 | tf_op jit(solution)/shard_map/while/body/eval_jaxpr/psum | solution.py:52
  134.7 3.1 copy.53
  141.2 5.9 %multiply_subtract_fusion.2 = f32[16,896,128]{2,1,0:T(8,128)} fusion(f32[16,896,128]{2,1,0:T(8,128)S(1)} %copy.53, f32[16,896,128]{2,1,0:T(8,128)S(1)} %copy-done.1, f32[896,128]{1,0:T(8,128)S(1)} %get-tuple-element.185, f32[16,896]{1,0:T(8,128)S(1)} %fusion.47, bf16[16,128,128]{2,1,0:T(8,128)(2,1)S(1)} %get-tuple-element.183), kind=kOutput, calls=%fused_computation.2.clone.1 | convolution fusion | flops 482607104 | bytes 23060480 | tf_op jit(solution)/shard_map/while/body/eval_jaxpr/svi,sij->svj/dot_general | solution.py:49
  148.1 15.8 %psum.25 = f32[16,350]{1,0:T(8,128)S(1)} all-reduce(f32[16,350]{1,0:T(8,128)S(1)} %fusion.48), channel_id=1, replica_groups=mesh['scen'=8,'veh'=4] {'veh'}, use_global_device_ids=true, to_apply=%region_2.0 | all-reduce | flops 5600 | bytes 44800 | tf_op jit(solution)/shard_map/while/body/eval_jaxpr/psum | solution.py:52
  163.9 3.1 copy.53
  170.5 5.9 %multiply_subtract_fusion.2 = f32[16,896,128]{2,1,0:T(8,128)} fusion(f32[16,896,128]{2,1,0:T(8,128)S(1)} %copy.53, f32[16,896,128]{2,1,0:T(8,128)S(1)} %copy-done.1, f32[896,128]{1,0:T(8,128)S(1)} %get-tuple-element.185, f32[16,896]{1,0:T(8,128)S(1)} %fusion.47, bf16[16,128,128]{2,1,0:T(8,128)(2,1)S(1)} %get-tuple-element.183), kind=kOutput, calls=%fused_computation.2.clone.1 | convolution fusion | flops 482607104 | bytes 23060480 | tf_op jit(solution)/shard_map/while/body/eval_jaxpr/svi,sij->svj/dot_general | solution.py:49
  177.3 17.4 %psum.25 = f32[16,350]{1,0:T(8,128)S(1)} all-reduce(f32[16,350]{1,0:T(8,128)S(1)} %fusion.48), channel_id=1, replica_groups=mesh['scen'=8,'veh'=4] {'veh'}, use_global_device_ids=true, to_apply=%region_2.0 | all-reduce | flops 5600 | bytes 44800 | tf_op jit(solution)/shard_map/while/body/eval_jaxpr/psum | solution.py:52
  194.8 3.1 copy.53
  201.3 5.9 %multiply_subtract_fusion.2 = f32[16,896,128]{2,1,0:T(8,128)} fusion(f32[16,896,128]{2,1,0:T(8,128)S(1)} %copy.53, f32[16,896,128]{2,1,0:T(8,128)S(1)} %copy-done.1, f32[896,128]{1,0:T(8,128)S(1)} %get-tuple-element.185, f32[16,896]{1,0:T(8,128)S(1)} %fusion.47, bf16[16,128,128]{2,1,0:T(8,128)(2,1)S(1)} %get-tuple-element.183), kind=kOutput, calls=%fused_computation.2.clone.1 | convolution fusion | flops 482607104 | bytes 23060480 | tf_op jit(solution)/shard_map/while/body/eval_jaxpr/svi,sij->svj/dot_general | solution.py:49
  208.2 16.0 %psum.25 = f32[16,350]{1,0:T(8,128)S(1)} all-reduce(f32[16,350]{1,0:T(8,128)S(1)} %fusion.48), channel_id=1, replica_groups=mesh['scen'=8,'veh'=4] {'veh'}, use_global_device_ids=true, to_apply=%region_2.0 | all-reduce | flops 5600 | bytes 44800 | tf_op jit(solution)/shard_map/while/body/eval_jaxpr/psum | solution.py:52
  224.2 3.1 copy.53
  230.7 5.9 %multiply_subtract_fusion.2 = f32[16,896,128]{2,1,0:T(8,128)} fusion(f32[16,896,128]{2,1,0:T(8,128)S(1)} %copy.53, f32[16,896,128]{2,1,0:T(8,128)S(1)} %copy-done.1, f32[896,128]{1,0:T(8,128)S(1)} %get-tuple-element.185, f32[16,896]{1,0:T(8,128)S(1)} %fusion.47, bf16[16,128,128]{2,1,0:T(8,128)(2,1)S(1)} %get-tuple-element.183), kind=kOutput, calls=%fused_computation.2.clone.1 | convolution fusion | flops 482607104 | bytes 23060480 | tf_op jit(solution)/shard_map/while/body/eval_jaxpr/svi,sij->svj/dot_general | solution.py:49
  237.5 17.3 %psum.25 = f32[16,350]{1,0:T(8,128)S(1)} all-reduce(f32[16,350]{1,0:T(8,128)S(1)} %fusion.48), channel_id=1, replica_groups=mesh['scen'=8,'veh'=4] {'veh'}, use_global_device_ids=true, to_apply=%region_2.0 | all-reduce | flops 5600 | bytes 44800 | tf_op jit(solution)/shard_map/while/body/eval_jaxpr/psum | solution.py:52
  254.9 3.1 copy.53
  261.4 5.9 %multiply_subtract_fusion.2 = f32[16,896,128]{2,1,0:T(8,128)} fusion(f32[16,896,128]{2,1,0:T(8,128)S(1)} %copy.53, f32[16,896,128]{2,1,0:T(8,128)S(1)} %copy-done.1, f32[896,128]{1,0:T(8,128)S(1)} %get-tuple-element.185, f32[16,896]{1,0:T(8,128)S(1)} %fusion.47, bf16[16,128,128]{2,1,0:T(8,128)(2,1)S(1)} %get-tuple-element.183), kind=kOutput, calls=%fused_computation.2.clone.1 | convolution fusion | flops 482607104 | bytes 23060480 | tf_op jit(solution)/shard_map/while/body/eval_jaxpr/svi,sij->svj/dot_general | solution.py:49
  268.3 16.1 %psum.25 = f32[16,350]{1,0:T(8,128)S(1)} all-reduce(f32[16,350]{1,0:T(8,128)S(1)} %fusion.48), channel_id=1, replica_groups=mesh['scen'=8,'veh'=4] {'veh'}, use_global_device_ids=true, to_apply=%region_2.0 | all-reduce | flops 5600 | bytes 44800 | tf_op jit(solution)/shard_map/while/body/eval_jaxpr/psum | solution.py:52
  284.4 3.1 copy.53
  291.0 5.9 %multiply_subtract_fusion.2 = f32[16,896,128]{2,1,0:T(8,128)} fusion(f32[16,896,128]{2,1,0:T(8,128)S(1)} %copy.53, f32[16,896,128]{2,1,0:T(8,128)S(1)} %copy-done.1, f32[896,128]{1,0:T(8,128)S(1)} %get-tuple-element.185, f32[16,896]{1,0:T(8,128)S(1)} %fusion.47, bf16[16,128,128]{2,1,0:T(8,128)(2,1)S(1)} %get-tuple-element.183), kind=kOutput, calls=%fused_computation.2.clone.1 | convolution fusion | flops 482607104 | bytes 23060480 | tf_op jit(solution)/shard_map/while/body/eval_jaxpr/svi,sij->svj/dot_general | solution.py:49
  297.8 17.1 %psum.25 = f32[16,350]{1,0:T(8,128)S(1)} all-reduce(f32[16,350]{1,0:T(8,128)S(1)} %fusion.48), channel_id=1, replica_groups=mesh['scen'=8,'veh'=4] {'veh'}, use_global_device_ids=true, to_apply=%region_2.0 | all-reduce | flops 5600 | bytes 44800 | tf_op jit(solution)/shard_map/while/body/eval_jaxpr/psum | solution.py:52
  315.0 3.1 copy.53
  321.5 5.9 %multiply_subtract_fusion.2 = f32[16,896,128]{2,1,0:T(8,128)} fusion(f32[16,896,128]{2,1,0:T(8,128)S(1)} %copy.53, f32[16,896,128]{2,1,0:T(8,128)S(1)} %copy-done.1, f32[896,128]{1,0:T(8,128)S(1)} %get-tuple-element.185, f32[16,896]{1,0:T(8,128)S(1)} %fusion.47, bf16[16,128,128]{2,1,0:T(8,128)(2,1)S(1)} %get-tuple-element.183), kind=kOutput, calls=%fused_computation.2.clone.1 | convolution fusion | flops 482607104 | bytes 23060480 | tf_op jit(solution)/shard_map/while/body/eval_jaxpr/svi,sij->svj/dot_general | solution.py:49
  328.4 16.2 %psum.25 = f32[16,350]{1,0:T(8,128)S(1)} all-reduce(f32[16,350]{1,0:T(8,128)S(1)} %fusion.48), channel_id=1, replica_groups=mesh['scen'=8,'veh'=4] {'veh'}, use_global_device_ids=true, to_apply=%region_2.0 | all-reduce | flops 5600 | bytes 44800 | tf_op jit(solution)/shard_map/while/body/eval_jaxpr/psum | solution.py:52
  344.6 3.1 copy.53
  351.1 5.9 %multiply_subtract_fusion.2 = f32[16,896,128]{2,1,0:T(8,128)} fusion(f32[16,896,128]{2,1,0:T(8,128)S(1)} %copy.53, f32[16,896,128]{2,1,0:T(8,128)S(1)} %copy-done.1, f32[896,128]{1,0:T(8,128)S(1)} %get-tuple-element.185, f32[16,896]{1,0:T(8,128)S(1)} %fusion.47, bf16[16,128,128]{2,1,0:T(8,128)(2,1)S(1)} %get-tuple-element.183), kind=kOutput, calls=%fused_computation.2.clone.1 | convolution fusion | flops 482607104 | bytes 23060480 | tf_op jit(solution)/shard_map/while/body/eval_jaxpr/svi,sij->svj/dot_general | solution.py:49
  358.0 17.1 %psum.25 = f32[16,350]{1,0:T(8,128)S(1)} all-reduce(f32[16,350]{1,0:T(8,128)S(1)} %fusion.48), channel_id=1, replica_groups=mesh['scen'=8,'veh'=4] {'veh'}, use_global_device_ids=true, to_apply=%region_2.0 | all-reduce | flops 5600 | bytes 44800 | tf_op jit(solution)/shard_map/while/body/eval_jaxpr/psum | solution.py:52
  375.1 3.1 copy.53
  381.6 5.9 %multiply_subtract_fusion.2 = f32[16,896,128]{2,1,0:T(8,128)} fusion(f32[16,896,128]{2,1,0:T(8,128)S(1)} %copy.53, f32[16,896,128]{2,1,0:T(8,128)S(1)} %copy-done.1, f32[896,128]{1,0:T(8,128)S(1)} %get-tuple-element.185, f32[16,896]{1,0:T(8,128)S(1)} %fusion.47, bf16[16,128,128]{2,1,0:T(8,128)(2,1)S(1)} %get-tuple-element.183), kind=kOutput, calls=%fused_computation.2.clone.1 | convolution fusion | flops 482607104 | bytes 23060480 | tf_op jit(solution)/shard_map/while/body/eval_jaxpr/svi,sij->svj/dot_general | solution.py:49
  388.5 16.2 %psum.25 = f32[16,350]{1,0:T(8,128)S(1)} all-reduce(f32[16,350]{1,0:T(8,128)S(1)} %fusion.48), channel_id=1, replica_groups=mesh['scen'=8,'veh'=4] {'veh'}, use_global_device_ids=true, to_apply=%region_2.0 | all-reduce | flops 5600 | bytes 44800 | tf_op jit(solution)/shard_map/while/body/eval_jaxpr/psum | solution.py:52
  404.8 14.0 %fusion.14 = f32[8,896,128]{2,0,1:T(8,128)} fusion(f32[16,896,128]{2,1,0:T(8,128)} %get-tuple-element.48, f32[16]{0:T(128)S(1)} %dynamic-slice_convert_fusion.1, s32[16]{0:T(128)S(1)} %dynamic-slice_bitcast_fusion), kind=kOutput, calls=%fused_computation.18 | convolution fusion | flops 176161024 | bytes 11010176 | tf_op jit(solution)/shard_map/sb,svi->bvi/dot_general | solution.py:71
  418.8 5.6 convert_element_type.49
  425.8 67.3 %all-reduce.2.cloned.1.call-done = f32[8,896,128]{2,0,1:T(8,128)} async-done(((f32[8,896,128]{2,0,1:T(8,128)}), f32[8,896,128]{2,0,1:T(8,128)}) %all-reduce.2.cloned.1.call-update) | async-done | bytes 3670032 | tf_op jit(solution)/shard_map/psum | solution.py:72
  493.1 2.5 broadcast_divide_fusion
  496.2 17.2 %multiply_reduce_fusion.1 = (f32[16]{0:T(128)S(1)}, bf16[16,896,128]{2,0,1:T(8,128)(2,1)S(1)}) fusion(bf16[16,896,128]{2,1,0:T(8,128)(2,1)S(1)} %copy-done.3, f32[8,896,128]{2,0,1:T(8,128)S(1)} %broadcast_divide_fusion, s32[16]{0:T(128)S(1)} %dynamic-slice_bitcast_fusion, f32[16,896,128]{2,1,0:T(8,128)} %get-tuple-element.48), kind=kOutput, calls=%fused_computation.17 | convolution fusion | flops 187170928 | bytes 18350208 | tf_op jit(solution)/shard_map/sb,bvi->svi/dot_general | solution.py:75
  514.1 2.8 copy.30
  516.9 39.5 %psum.22 = f32[]{:T(128)} all-reduce(f32[]{:T(128)} %multiply_reduce_fusion.2), channel_id=1, replica_groups=mesh['scen'=8,'veh'=4] {'scen','veh'}, use_global_device_ids=true, to_apply=%region_8.0 | all-reduce | flops 1 | bytes 8 | tf_op jit(solution)/shard_map/psum | solution.py:79
  557.1 2.4 dynamic-slice_convert_fusion
  (106 shorter events, 57.5 us)
Async XLA Ops:
  7.2 1.5 copy-start
  7.2 485.9 %all-reduce.2.cloned.1.call-start = ((), (), s32[]{:S(2)}) async-start(), calls=%async_computation | async-start | bytes 7340032 | tf_op jit(solution)/shard_map/psum | solution.py:72
  31.3 5.2 copy-start.5
  36.5 3.8 copy-start.9
  36.5 3.8 copy-start.4
  36.5 3.9 copy-start.7
  36.5 3.9 copy-start.8
  36.5 3.9 copy-start.11
  40.4 364.3 %copy-start.10 = (s32[128]{0:T(128)S(1)}, s32[128]{0:T(128)}, u32[]{:S(2)}) copy-start(s32[128]{0:T(128)} %param.23) | copy-start | bytes 1540
  43.5 3.5 copy-start.1
  77.7 3.5 copy-start.1
  106.9 3.5 copy-start.1
  137.8 3.5 copy-start.1
  167.0 3.5 copy-start.1
  197.9 3.5 copy-start.1
  227.2 3.5 copy-start.1
  258.0 3.5 copy-start.1
  287.5 3.5 copy-start.1
  318.1 3.5 copy-start.1
  347.7 3.5 copy-start.1
  378.1 3.5 copy-start.1
  404.7 14.1 %copy-start.6 = (f32[16,350]{1,0:T(8,128)}, f32[16,350]{1,0:T(8,128)S(1)}, u32[]{:S(2)}) copy-start(f32[16,350]{1,0:T(8,128)S(1)} %get-tuple-element.93) | copy-start | bytes 67204
  418.7 6.9 %copy-start.12 = (s32[128,1]{0,1:T(1,128)S(1)}, s32[128,1]{0,1:T(1,128)}, u32[]{:S(2)}) copy-start(s32[128,1]{0,1:T(1,128)} %param.22) | copy-start | bytes 1540
  493.1 3.1 copy-start.3
  496.2 17.2 %copy-start.2 = (f32[8,896,128]{2,0,1:T(8,128)}, f32[8,896,128]{2,0,1:T(8,128)S(1)}, u32[]{:S(2)}) copy-start(f32[8,896,128]{2,0,1:T(8,128)S(1)} %broadcast_divide_fusion) | copy-start | bytes 11010052
Sparse Core Ops, SparseCore 0:
  418.9 74.1 all-reduce.1
where the time goes:
time: 569 us; the launch traced here: 568 us
  blocking collectives  243 us (43%)
  matrix products  152 us (27%)
  waiting for transfers between devices  67.3 us (12%)
  local copies, waits for them, and re-layouts  50.3 us (9%)
  other arithmetic  38.6 us (7%)
  between operations  16.7 us (3%)
    psum x12, blocking collectives, advance(): usage = lax.psum(partial_use, 'veh')  203 us
    dot_general x12, matrix products, advance(): jnp.einsum('svi,sij->svj', rounded, hessian, preferred_element_type=jnp.f...  70.6 us
    psum x1, waiting for transfers between devices, shards(): totals = lax.psum(partial_sums, 'scen')  67.3 us
    psum x1, blocking collectives, shards(): spread_total = lax.psum(spread, ('scen', 'veh'))  39.5 us
    while x36, local copies, waits for them, and re-layouts  37.1 us
    reduce_sum x12, other arithmetic, advance(): consumed = jnp.sum(roster * coefficient[None], axis=2)  25.1 us
    dot_general x1, matrix products, shards(): jnp.einsum('sb,bvi->svi', selector.astype(jnp.bfloat16), anchor, preferre...  22.6 us
    dot_general x1, matrix products, shards(): jnp.einsum('sb,bvi->svi', selector, every_mean, precision=highest)  17.2 us
  transfers between devices with their start and end apart: 1, of which 1 were waited for; matrix products, arithmetic and copies ran while one was open for 1% of the time, Pallas kernels for 0%

commit v1 on v0

v1 whole, which is shorter than its diff:
```python
import functools

import jax
import jax.numpy as jnp
from jax import lax
from jax.experimental import pallas as pl
from jax.experimental.pallas import tpu as pltpu
from jax.sharding import PartitionSpec as P

ITERS = 12


penalty = 1.0
step_size = 0.02
dual_step = 0.02
highest = lax.Precision.HIGHEST
MESH = pl.DeviceIdType.MESH
LANES = 128


def halves(x):
    high = x.astype(jnp.bfloat16)
    return high, (x - high.astype(jnp.float32)).astype(jnp.bfloat16)


def steps_kernel(
    n,
    bundle_ref,
    start_ref,
    cost_ref,
    price_ref,
    anchor_ref,
    hess_ref,
    coef_ref,
    limit_ref,
    dual_ref,
    crew_ref,
    roster_ref,
    dual_out_ref,
    linear_ref,
    wide_ref,
    map_ref,
    coef_wide_ref,
    picked_ref,
    eaten_ref,
    use_ref,
    send_sem,
    recv_sem,
):
    me = lax.axis_index("veh")
    scen, rows, width = start_ref.shape
    crews = map_ref.shape[1]
    chunk = 64 if rows % 64 == 0 else rows

    barrier = pltpu.get_barrier_semaphore()
    for off in range(1, n):
        pl.semaphore_signal(
            barrier, inc=1, device_id={"veh": lax.rem(me + off, n)}, device_id_type=MESH
        )
    pl.semaphore_wait(barrier, n - 1)

    def outgoing(k, off):
        return pltpu.make_async_remote_copy(
            src_ref=use_ref.at[k, me],
            dst_ref=use_ref.at[k, me],
            send_sem=send_sem.at[k, off - 1],
            recv_sem=recv_sem.at[k, off - 1],
            device_id={"veh": lax.rem(me + off, n)},
            device_id_type=MESH,
        )

    def incoming(k, off):
        source = lax.rem(me + n - off, n)
        return pltpu.make_async_remote_copy(
            src_ref=use_ref.at[k, source],
            dst_ref=use_ref.at[k, source],
            send_sem=send_sem.at[k, off - 1],
            recv_sem=recv_sem.at[k, off - 1],
            device_id={"veh": lax.rem(me + off, n)},
            device_id_type=MESH,
        )

    map_ref[...] = jnp.where(
        crew_ref[...] == lax.broadcasted_iota(jnp.int32, (rows, crews), 1), 1.0, 0.0
    ).astype(jnp.bfloat16)
    coef_wide_ref[...] = coef_ref[...].astype(jnp.float32)
    eaten_ref[...] = jnp.zeros_like(eaten_ref)
    picked_ref[...] = jnp.zeros_like(picked_ref)
    dual_out_ref[...] = dual_ref[...]

    def lane_is(s):
        lanes = lax.broadcasted_iota(jnp.int32, (chunk, LANES), 1)
        return (lanes == s) | (lanes == s + scen)

    def prepare(s, carry):
        wide_ref[s, 0:width, 0:width] = hess_ref[s]
        wide_ref[s, 0:width, width:] = jnp.zeros((width, LANES), jnp.bfloat16)
        wide_ref[s, width:, 0:width] = jnp.zeros((LANES, width), jnp.bfloat16)
        row = lax.broadcasted_iota(jnp.int32, (LANES, LANES), 0)
        wide_ref[s, width:, width:] = jnp.where(
            (row == s) | (row == s + scen), 1.0, 0.0
        ).astype(jnp.bfloat16)
        mine = bundle_ref[s]
        mask = lane_is(s)
        for lo in range(0, rows, chunk):
            part = slice(lo, lo + chunk)
            linear_ref[s, part] = (
                cost_ref[s, part].astype(jnp.float32)
                + price_ref[s, part].astype(jnp.float32)
                - penalty * anchor_ref[mine, part].astype(jnp.float32)
            )
            roster = start_ref[s, part].astype(jnp.float32)
            roster_ref[s, part] = roster
            eaten = jnp.sum(roster * coef_wide_ref[part], axis=1, keepdims=True)
            eaten_ref[part] = jnp.where(mask, eaten, eaten_ref[part])
        return carry

    def share(k):
        high, low = halves(eaten_ref[...])
        lanes = lax.broadcasted_iota(jnp.int32, high.shape, 1)
        both = jnp.where(
            lanes < scen, high.astype(jnp.float32), low.astype(jnp.float32)
        ).astype(jnp.bfloat16)
        summed = lax.dot_general(
            both, map_ref[...], (((0,), (0,)), ((), ())), preferred_element_type=jnp.float32
        )
        use_ref[k, me] = summed[0:scen] + summed[scen : 2 * scen]
        for off in range(1, n):
            outgoing(k, off).start()

    def collect(k):
        for off in range(1, n):
            incoming(k, off).wait_recv()
        usage = use_ref[k, 0]
        for other in range(1, n):
            usage = usage + use_ref[k, other]
        dual_out_ref[...] = jnp.maximum(
            dual_out_ref[...] + dual_step * (usage - limit_ref[...]), 0.0
        )

    lax.fori_loop(0, scen, prepare, 0)
    share(0)

    def advance(k, carry):
        @pl.when(k > 0)
        def _():
            collect(k - 1)

        high, low = halves(dual_out_ref[...])
        pieces = jnp.concatenate([high, low], axis=0)
        picked_ref[:, 0 : 2 * scen] = lax.dot_general(
            map_ref[...], pieces, (((1,), (1,)), ((), ())), preferred_element_type=jnp.float32
        ).astype(jnp.bfloat16)

        def one(s, inner):
            left = jnp.concatenate([roster_ref[s].astype(jnp.bfloat16), picked_ref[...]], axis=1)
            both = jnp.dot(left, wide_ref[s], preferred_element_type=jnp.float32)
            mask = lane_is(s)
            for lo in range(0, rows, chunk):
                part = slice(lo, lo + chunk)
                coef = coef_wide_ref[part]
                roster = roster_ref[s, part]
                gradient = (
                    both[part, 0:width]
                    + linear_ref[s, part]
                    + penalty * roster
                    + both[part, width:] * coef
                )
                roster = roster - step_size * gradient
                roster_ref[s, part] = roster
                eaten = jnp.sum(roster * coef, axis=1, keepdims=True)
                eaten_ref[part] = jnp.where(mask, eaten, eaten_ref[part])
            return inner

        lax.fori_loop(0, scen, one, 0)

        @pl.when(k < ITERS - 1)
        def _():
            share(k + 1)

        return carry

    lax.fori_loop(0, ITERS, advance, 0)
    collect(ITERS - 1)

    def drain(k, carry):
        for off in range(1, n):
            outgoing(k, off).wait_send()
        return carry

    lax.fori_loop(0, ITERS, drain, 0)


def run_steps(start_plan, linear_cost, price, anchor, hessian, usage_coef, crew_limit, crew_dual, crew_row, my_bundles):
    n = lax.axis_size("veh")
    scen, rows, width = start_plan.shape
    crew_count = crew_limit.shape[1]
    crews = -(-crew_count // LANES) * LANES
    extra = ((0, 0), (0, crews - crew_count))
    vmem = pl.BlockSpec(memory_space=pltpu.VMEM)
    roster, dual = pl.pallas_call(
        functools.partial(steps_kernel, n),
        out_shape=(
            jax.ShapeDtypeStruct((scen, rows, width), jnp.float32),
            jax.ShapeDtypeStruct((scen, crews), jnp.float32),
        ),
        in_specs=[pl.BlockSpec(memory_space=pltpu.SMEM)] + [vmem] * 9,
        out_specs=(vmem, vmem),
        scratch_shapes=[
            pltpu.VMEM((scen, rows, width), jnp.float32),
            pltpu.VMEM((scen, width + LANES, width + LANES), jnp.bfloat16),
            pltpu.VMEM((rows, crews), jnp.bfloat16),
            pltpu.VMEM((rows, width), jnp.float32),
            pltpu.VMEM((rows, LANES), jnp.bfloat16),
            pltpu.VMEM((rows, LANES), jnp.float32),
            pltpu.VMEM((ITERS, n, scen, crews), jnp.float32),
            pltpu.SemaphoreType.DMA((ITERS, n - 1)),
            pltpu.SemaphoreType.DMA((ITERS, n - 1)),
        ],
        compiler_params=pltpu.CompilerParams(
            collective_id=0, has_side_effects=True, vmem_limit_bytes=62 * 1024 * 1024
        ),
    )(
        my_bundles,
        start_plan,
        linear_cost,
        price,
        anchor,
        hessian,
        usage_coef,
        jnp.pad(crew_limit, extra),
        jnp.pad(crew_dual, extra),
        crew_row[:, None],
    )
    return roster, dual[:, :crew_count]


def bit_of(index, bit):
    return lax.rem(lax.div(index, 2**bit), 2)


def spans(bits):
    out = [0]
    for bit in bits:
        out = out + [value + 2**bit for value in out]
    return out


def consensus_kernel(
    n_scen,
    n_veh,
    pieces,
    bundle_ref,
    pick_ref,
    weight_ref,
    every_ref,
    scale_ref,
    roster_ref,
    price_ref,
    plan_out,
    price_out,
    mean_out,
    gap_out,
    part_ref,
    land_ref,
    spread_ref,
    near_ref,
    far_ref,
    send_sem,
    recv_sem,
    side_send,
    side_recv,
    *mean_refs,
):
    me = lax.axis_index("scen")
    my_veh = lax.axis_index("veh")
    scen, rows, width = roster_ref.shape
    owned = mean_out.shape[0]
    bundles = part_ref.shape[0]
    bits = n_scen.bit_length() - 1
    size = rows // pieces
    half = size // 2 if size % 16 == 0 else size
    plain = list(range(bits))
    turned = plain[:1] + plain[:0:-1]

    barrier = pltpu.get_barrier_semaphore()
    for off in range(1, n_scen):
        pl.semaphore_signal(
            barrier, inc=1, device_id={"scen": lax.rem(me + off, n_scen)}, device_id_type=MESH
        )
    for off in range(1, n_veh):
        pl.semaphore_signal(
            barrier, inc=1, device_id={"veh": lax.rem(my_veh + off, n_veh)}, device_id_type=MESH
        )
    pl.semaphore_wait(barrier, n_scen + n_veh - 2)

    def partner(bit):
        return me + 2**bit - 2 ** (bit + 1) * bit_of(me, bit)

    def base_of(index, free):
        value = index
        for bit in free:
            value = value - 2**bit * bit_of(index, bit)
        return value

    def part_of(q):
        return pl.ds(q * size, size)

    def copies(q, stage):
        order = plain if q % 2 == 0 else turned
        down = stage < bits
        level = stage if down else 2 * bits - 1 - stage
        bit = order[level]
        free = order[level + 1 :]
        offsets = spans(free)
        found = []
        slot = sum(2 ** (bits - 1 - earlier) for earlier in range(level))
        for place, offset in enumerate(offsets):
            sem = (q * 2 + (0 if down else 1)) * (n_scen - 1) + slot + place
            other = partner(bit)
            if down:
                target = (base_of(other, free) + offset) * owned
                source = part_ref.at[pl.ds(target, owned), part_of(q)]
                goal = land_ref.at[slot + place, :, part_of(q)]
                mine = goal
            else:
                held = (base_of(me, free) + offset) * owned
                theirs = (base_of(other, free) + offset) * owned
                source = mean_refs[q].at[pl.ds(held, owned)]
                goal = source
                mine = mean_refs[q].at[pl.ds(theirs, owned)]
            out = functools.partial(
                pltpu.make_async_remote_copy,
                src_ref=source,
                dst_ref=goal,
                send_sem=send_sem.at[sem],
                recv_sem=recv_sem.at[sem],
                device_id={"scen": other},
                device_id_type=MESH,
            )
            back = functools.partial(
                pltpu.make_async_remote_copy,
                src_ref=source,
                dst_ref=mine,
                send_sem=send_sem.at[sem],
                recv_sem=recv_sem.at[sem],
                device_id={"scen": other},
                device_id_type=MESH,
            )
            keep = (base_of(me, free) + offset) * owned
            found.append((out, back, slot + place, keep))
        return found

    def launch(q, stage):
        for out, _, _, _ in copies(q, stage):
            out().start()

    def absorb(q, stage):
        for _, back, slot, keep in copies(q, stage):
            back().wait_recv()
            if stage < bits:
                for one in range(owned):
                    part_ref[keep + one, part_of(q)] += land_ref[slot, one, part_of(q)]

    def sums(q):
        def one(b, carry):
            for lo in range(0, size, half):
                where = pl.ds(q * size + lo, half)
                total = pick_ref[b, 0] * roster_ref[0, where]
                for s in range(1, scen):
                    total = total + pick_ref[b, s] * roster_ref[s, where]
                part_ref[b, where] = total
            return carry

        lax.fori_loop(0, bundles, one, 0)

    def settle(q):
        for one in range(owned):
            b = me * owned + one
            mean = part_ref[b, part_of(q)] / every_ref[b]
            mean_refs[q][b] = mean
            mean_out[one, part_of(q)] = mean.astype(jnp.bfloat16)

    def finish(q):
        def one(s, total):
            roster = roster_ref[s, part_of(q)]
            deviation = roster - mean_refs[q][bundle_ref[s]]
            plan_out[s, part_of(q)] = roster.astype(jnp.bfloat16)
            price_out[s, part_of(q)] = (
                price_ref[s, part_of(q)].astype(jnp.float32) + penalty * deviation
            ).astype(jnp.bfloat16)
            square = jnp.sum((deviation * deviation).reshape(size // 8, 8, width), axis=0)
            return total + weight_ref[s] * square

        spread_ref[...] = lax.fori_loop(0, scen, one, spread_ref[...])

    spread_ref[...] = jnp.zeros_like(spread_ref)
    for turn in range(pieces + 2 * bits):
        for stage in range(2 * bits + 1):
            q = turn - stage
            if q < 0 or q >= pieces:
                continue
            if stage == 0:
                sums(q)
            else:
                absorb(q, stage - 1)
            if stage == bits:
                settle(q)
            if stage < 2 * bits:
                launch(q, stage)
            else:
                finish(q)

    near_ref[me] = spread_ref[...]
    steps = []
    for axis, here, count, ref, first in (
        ("scen", me, n_scen, near_ref, 0),
        ("veh", my_veh, n_veh, far_ref, n_scen - 1),
    ):
        sent = []
        if axis == "veh":
            total = near_ref[0]
            for other in range(1, n_scen):
                total = total + near_ref[other]
            far_ref[my_veh] = total
        for off in range(1, count):
            sem = first + off - 1
            out = pltpu.make_async_remote_copy(
                src_ref=ref.at[here],
                dst_ref=ref.at[here],
                send_sem=side_send.at[sem],
                recv_sem=side_recv.at[sem],
                device_id={axis: lax.rem(here + off, count)},
                device_id_type=MESH,
            )
            out.start()
            sent.append(out)
        for off in range(1, count):
            sem = first + off - 1
            origin = lax.rem(here + count - off, count)
            pltpu.make_async_remote_copy(
                src_ref=ref.at[origin],
                dst_ref=ref.at[origin],
                send_sem=side_send.at[sem],
                recv_sem=side_recv.at[sem],
                device_id={axis: lax.rem(here + off, count)},
                device_id_type=MESH,
            ).wait_recv()
        steps = steps + sent
    total = far_ref[0]
    for other in range(1, n_veh):
        total = total + far_ref[other]
    whole = jnp.sum(jnp.sum(total, axis=1, keepdims=True), axis=0, keepdims=True)
    gap_out[...] = jnp.sqrt(jnp.broadcast_to(whole, gap_out.shape) / scale_ref[0])

    for out in steps:
        out.wait_send()
    for q in range(pieces):
        for stage in range(2 * bits):
            for out, _, _, _ in copies(q, stage):
                out().wait_send()


def run_consensus(roster, price, my_bundles, pick, my_weights, every_weight, scale, bundles):
    n_scen, n_veh = lax.axis_size("scen"), lax.axis_size("veh")
    scen, rows, width = roster.shape
    owned = bundles // n_scen
    pieces = 8
    while rows % (8 * pieces):
        pieces = pieces // 2
    vmem = pl.BlockSpec(memory_space=pltpu.VMEM)
    smem = pl.BlockSpec(memory_space=pltpu.SMEM)
    copies = pieces * 2 * (n_scen - 1)
    side = n_scen + n_veh - 2
    f32, bf16 = jnp.float32, jnp.bfloat16
    return pl.pallas_call(
        functools.partial(consensus_kernel, n_scen, n_veh, pieces),
        out_shape=(
            jax.ShapeDtypeStruct((scen, rows, width), bf16),
            jax.ShapeDtypeStruct((scen, rows, width), bf16),
            jax.ShapeDtypeStruct((owned, rows, width), bf16),
            jax.ShapeDtypeStruct((8, LANES), f32),
        ),
        in_specs=[smem] * 5 + [vmem] * 2,
        out_specs=(vmem,) * 4,
        scratch_shapes=[
            pltpu.VMEM((bundles, rows, width), f32),
            pltpu.VMEM((n_scen - 1, owned, rows, width), f32),
            pltpu.VMEM((8, width), f32),
            pltpu.VMEM((n_scen, 8, width), f32),
            pltpu.VMEM((n_veh, 8, width), f32),
            pltpu.SemaphoreType.DMA((copies,)),
            pltpu.SemaphoreType.DMA((copies,)),
            pltpu.SemaphoreType.DMA((side,)),
            pltpu.SemaphoreType.DMA((side,)),
        ]
        + [pltpu.VMEM((bundles, rows // pieces, width), f32)] * pieces,
        compiler_params=pltpu.CompilerParams(
            collective_id=1, has_side_effects=True, vmem_limit_bytes=62 * 1024 * 1024
        ),
    )(my_bundles, pick, my_weights, every_weight, scale, roster, price)


def shards(
    start_plan,
    linear_cost,
    price,
    anchor,
    hessian,
    usage_coef,
    crew_limit,
    crew_dual,
    crew_row,
    bundle_of,
    scen_weight,
):
    local_scen = start_plan.shape[0]
    bundle_count = anchor.shape[0]
    offset = lax.axis_index("scen") * local_scen
    all_bundles = bundle_of[:, 0]
    my_bundles = lax.dynamic_slice_in_dim(all_bundles, offset, local_scen)
    my_weights = lax.dynamic_slice_in_dim(scen_weight, offset, local_scen).astype(jnp.float32)
    bundle_ids = jnp.arange(bundle_count, dtype=jnp.int32)
    selector = (my_bundles[:, None] == bundle_ids[None, :]).astype(jnp.float32)

    roster, multiplier = run_steps(
        start_plan, linear_cost, price, anchor, hessian, usage_coef,
        crew_limit, crew_dual, crew_row, my_bundles,
    )
    weighted_pick = selector * my_weights[:, None]
    every_weight = jnp.sum(
        (all_bundles[:, None] == bundle_ids[None, :]).astype(jnp.float32)
        * scen_weight.astype(jnp.float32)[:, None],
        axis=0,
    )
    entries = start_plan.shape[1] * lax.axis_size("veh") * start_plan.shape[2]
    scale = (jnp.sum(scen_weight.astype(jnp.float32)) * entries)[None]
    plan, new_price, own_mean, gap = run_consensus(
        roster, price, my_bundles, weighted_pick.T, my_weights, every_weight, scale, bundle_count
    )
    return (plan, new_price, own_mean, multiplier, gap[0, 0])


def solution(mesh):
    return jax.shard_map(
        shards,
        mesh=mesh,
        in_specs=(
            P("scen", "veh", None),
            P("scen", "veh", None),
            P("scen", "veh", None),
            P(None, "veh", None),
            P("scen", None, None),
            P("veh", None),
            P("scen", None),
            P("scen", None),
            P("veh"),
            P(),
            P(),
        ),
        out_specs=(
            P("scen", "veh", None),
            P("scen", "veh", None),
            P("scen", "veh", None),
            P("scen", None),
            P(),
        ),
        check_vma=False,
    )
```

time: 569 us -> 179 us (0.31)
  blocking collectives: 243 us -> 0 us
  Pallas kernels: 0 us -> 159 us
  matrix products: 152 us -> 0 us
  waiting for transfers between devices: 67.3 us -> 0 us
  local copies, waits for them, and re-layouts: 50.3 us -> 13.8 us
  other arithmetic: 38.6 us -> 4.58 us
  between operations: 16.7 us -> 1.32 us
    psum x13 -> x0, blocking collectives: 243 us -> none  [the longest x12 203 us: advance(): usage = lax.psum(partial_use, 'veh')]
    pallas_call x0 -> x2, Pallas kernels: none -> 159 us  [the longest x1 96.3 us: run_steps(): pl.pallas_call(functools.partial(steps_kernel, n), out_shape=(jax.ShapeDt...]
    dot_general x39 -> x0, matrix products: 152 us -> none  [the longest x12 70.6 us: advance(): jnp.einsum('svi,sij->svj', rounded, hessian, preferred_element_type=jnp.f...]
    psum x1 -> x0, waiting for transfers between devices: 67.3 us -> none  [shards(): totals = lax.psum(partial_sums, 'scen')]
    while x36 -> x0, local copies, waits for them, and re-layouts: 37.1 us -> none
    reduce_sum x14 -> x1, other arithmetic: 26.4 us -> 1.26 us  [shards(): scale = (jnp.sum(scen_weight.astype(jnp.float32)) * entries)[None]]
    convert_element_type x3 -> x0, other arithmetic: 9.41 us -> none  [the longest x1 5.61 us: shards(): roster.astype(jnp.bfloat16)]
  transfers between devices with their start and end apart: 1 -> 0, of which waited for: 1 -> 0; matrix products, arithmetic and copies ran while one was open for 1% -> 0% of each run, Pallas kernels for 0% -> 0%
where the time goes in v1:
time: 179 us
  Pallas kernels  159 us (89%)
  local copies, waits for them, and re-layouts  13.8 us (8%)
  other arithmetic  4.58 us (3%)
    pallas_call x1, Pallas kernels, run_steps(): pl.pallas_call(functools.partial(steps_kernel, n), out_shape=(jax.ShapeDt...  96.3 us
    pallas_call x1, Pallas kernels, run_consensus(): pl.pallas_call(functools.partial(consensus_kernel, n_scen, n_veh, pieces)...  62.5 us
    unnamed x14, local copies, waits for them, and re-layouts  7.53 us

profile of v1, /device:TPU:0, one launch (start us, length us, event | category | flops | bytes accessed | tf_op | source)
XLA Modules:
  0.0 178.5 jit_solution(8375907726170800642)
XLA Ops:
  0.6 1.3 convert_reduce_fusion
  2.5 0.7 dynamic-slice_bitcast_fusion.bundle_ref
  3.3 0.0 copy-start.3
  3.3 0.7 dynamic-slice_convert_fusion.weight_ref
  4.0 0.0 copy-start.4
  4.0 0.7 convert_element_type.13
  4.7 1.3 select_reduce_fusion.every_ref
  6.0 0.6 fusion.pick_ref
  6.6 1.3 pad.7.limit_ref
  8.0 1.3 pad.8.dual_ref
  9.3 1.6 broadcast_in_dim.6.crew_ref
  10.9 0.0 copy-done.3
  10.9 96.3 %shard_map.146 = (f32[16,896,128]{2,1,0:T(8,128)}, f32[16,384]{1,0:T(8,128)}) custom-call(s32[16]{0:T(128)} %copy-done.3, bf16[16,896,128]{2,1,0:T(8,128)(2,1)} %start_ref.1, bf16[16,896,128]{2,1,0:T(8,128)(2,1)} %cost_ref.1, bf16[16,896,128]{2,1,0:T(8,128)(2,1)} %price_ref.3, bf16[8,896,128]{2,1,0:T(8,128)(2,1)} %anchor_ref.1, ...), custom_call_target="tpu_custom_call" | custom-call | tf_op jit(solution)/shard_map/pallas_call | solution.py:201
  107.2 0.0 copy-done.4
  107.3 62.5 %shard_map.147 = (bf16[16,896,128]{2,1,0:T(8,128)(2,1)}, bf16[16,896,128]{2,1,0:T(8,128)(2,1)}, bf16[1,896,128]{2,1,0:T(8,128)(2,1)}, f32[8,128]{1,0:T(8,128)}) custom-call(s32[16]{0:T(128)} %copy-done.3, f32[8,16]{1,0:T(8,128)} %fusion.pick_ref, f32[16]{0:T(128)} %copy-done.4, f32[8]{0:T(128)} %select_reduce_fusion.every_ref, f32[1]{0:T(128)} %bitcast.2.scale_ref, ...), custom_call_target="tpu_custom_call" | custom-call | tf_op jit(solution)/shard_map/pallas_call | solution.py:476
  169.8 1.2 slice.7
  171.0 0.0 copy-start
  171.0 4.4 %copy.22 = bf16[16,896,128]{2,1,0:T(8,128)(2,1)} copy(bf16[16,896,128]{2,1,0:T(8,128)(2,1)} %get-tuple-element.22) | data formatting | bytes 7340032
  175.4 0.0 copy-done
  175.4 0.0 copy-start.1
  175.4 0.0 copy-start.2
  175.4 1.8 %copy.23 = bf16[16,896,128]{2,1,0:T(8,128)(2,1)} copy(bf16[16,896,128]{2,1,0:T(8,128)(2,1)S(1)} %copy-done) | data formatting | bytes 7340032
  177.2 0.0 copy-done.1
  177.2 0.7 copy.24
  177.9 0.0 copy-done.2
  177.9 0.6 copy.25
Async XLA Ops:
  3.3 7.7 %copy-start.3 = (s32[16]{0:T(128)}, s32[16]{0:T(128)S(1)}, u32[]{:S(2)}) copy-start(s32[16]{0:T(128)S(1)} %dynamic-slice_bitcast_fusion.bundle_ref) | copy-start | bytes 196
  4.0 103.2 %copy-start.4 = (f32[16]{0:T(128)}, f32[16]{0:T(128)S(1)}, u32[]{:S(2)}) copy-start(f32[16]{0:T(128)S(1)} %dynamic-slice_convert_fusion.weight_ref) | copy-start | bytes 196
  171.0 4.4 %copy-start = (bf16[16,896,128]{2,1,0:T(8,128)(2,1)S(1)}, bf16[16,896,128]{2,1,0:T(8,128)(2,1)}, u32[]{:S(2)}) copy-start(bf16[16,896,128]{2,1,0:T(8,128)(2,1)} %get-tuple-element.23) | copy-start | bytes 11010052
  175.4 1.8 %copy-start.1 = (bf16[1,896,128]{2,1,0:T(8,128)(2,1)S(1)}, bf16[1,896,128]{2,1,0:T(8,128)(2,1)}, u32[]{:S(2)}) copy-start(bf16[1,896,128]{2,1,0:T(8,128)(2,1)} %get-tuple-element.24) | copy-start | bytes 688132
  175.4 2.5 %copy-start.2 = (f32[16,384]{1,0:T(8,128)S(1)}, f32[16,384]{1,0:T(8,128)}, u32[]{:S(2)}) copy-start(f32[16,384]{1,0:T(8,128)} %get-tuple-element.15) | copy-start | bytes 73732

commit v2 on v1

--- a/solution.py
+++ b/solution.py
@@ -1,4 +1,5 @@
 import functools
+import math
 
 import jax
 import jax.numpy as jnp
@@ -16,6 +17,7 @@
 highest = lax.Precision.HIGHEST
 MESH = pl.DeviceIdType.MESH
 LANES = 128
+GROUP = 4
 
 
 def halves(x):
@@ -50,7 +52,8 @@
     me = lax.axis_index("veh")
     scen, rows, width = start_ref.shape
     crews = map_ref.shape[1]
-    chunk = 64 if rows % 64 == 0 else rows
+    together = math.gcd(scen, GROUP)
+    chunk = 32 if rows % 32 == 0 else rows
 
     barrier = pltpu.get_barrier_semaphore()
     for off in range(1, n):
@@ -152,27 +155,39 @@
             map_ref[...], pieces, (((1,), (1,)), ((), ())), preferred_element_type=jnp.float32
         ).astype(jnp.bfloat16)
 
-        def one(s, inner):
-            left = jnp.concatenate([roster_ref[s].astype(jnp.bfloat16), picked_ref[...]], axis=1)
-            both = jnp.dot(left, wide_ref[s], preferred_element_type=jnp.float32)
-            mask = lane_is(s)
+        def several(group, inner):
+            chosen = [group * together + extra for extra in range(together)]
+            results = [
+                jnp.dot(
+                    jnp.concatenate(
+                        [roster_ref[s].astype(jnp.bfloat16), picked_ref[...]], axis=1
+                    ),
+                    wide_ref[s],
+                    preferred_element_type=jnp.float32,
+                )
+                for s in chosen
+            ]
+            masks = [lane_is(s) for s in chosen]
             for lo in range(0, rows, chunk):
                 part = slice(lo, lo + chunk)
                 coef = coef_wide_ref[part]
-                roster = roster_ref[s, part]
-                gradient = (
-                    both[part, 0:width]
-                    + linear_ref[s, part]
-                    + penalty * roster
-                    + both[part, width:] * coef
-                )
-                roster = roster - step_size * gradient
-                roster_ref[s, part] = roster
-                eaten = jnp.sum(roster * coef, axis=1, keepdims=True)
-                eaten_ref[part] = jnp.where(mask, eaten, eaten_ref[part])
+                gathered = eaten_ref[part]
+                for s, both, mask in zip(chosen, results, masks):
+                    roster = roster_ref[s, part]
+                    gradient = (
+                        both[part, 0:width]
+                        + linear_ref[s, part]
+                        + penalty * roster
+                        + both[part, width:] * coef
+                    )
+                    roster = roster - step_size * gradient
+                    roster_ref[s, part] = roster
+                    eaten = jnp.sum(roster * coef, axis=1, keepdims=True)
+                    gathered = jnp.where(mask, eaten, gathered)
+                eaten_ref[part] = gathered
             return inner
 
-        lax.fori_loop(0, scen, one, 0)
+        lax.fori_loop(0, scen // together, several, 0)
 
         @pl.when(k < ITERS - 1)
         def _():

time: 179 us -> 149 us (0.83)
  Pallas kernels: 159 us -> 129 us
    pallas_call x1, Pallas kernels: 96.3 us -> 65.7 us  [run_steps(): pl.pallas_call(functools.partial(steps_kernel, n), out_shape=(jax.ShapeDt...]
where the time goes in v2:
time: 149 us
  Pallas kernels  129 us (87%)
  local copies, waits for them, and re-layouts  13.8 us (9%)
  other arithmetic  4.58 us (3%)
    pallas_call x1, Pallas kernels, run_steps(): pl.pallas_call(functools.partial(steps_kernel, n), out_shape=(jax.ShapeDt...  65.7 us
    pallas_call x1, Pallas kernels, run_consensus(): pl.pallas_call(functools.partial(consensus_kernel, n_scen, n_veh, pieces)...  63.2 us
    unnamed x14, local copies, waits for them, and re-layouts  7.53 us

profile of v2, /device:TPU:0, one launch (start us, length us, event | category | flops | bytes accessed | tf_op | source)
XLA Modules:
  0.0 148.6 jit_solution(983711223047431441)
XLA Ops:
  0.6 1.3 convert_reduce_fusion
  2.5 0.7 dynamic-slice_bitcast_fusion.bundle_ref
  3.3 0.0 copy-start.3
  3.3 0.7 dynamic-slice_convert_fusion.weight_ref
  4.0 0.0 copy-start.4
  4.0 0.7 convert_element_type.13
  4.7 1.3 select_reduce_fusion.every_ref
  6.0 0.6 fusion.pick_ref
  6.6 1.3 pad.7.limit_ref
  8.0 1.3 pad.8.dual_ref
  9.3 1.6 %broadcast_in_dim.6.crew_ref = s32[896,1]{1,0:T(8,128)} reshape(s32[896]{0:T(1024)} %param.19) | data formatting | bytes 7168 | tf_op jit(solution)/shard_map/broadcast_in_dim | solution.py:248
  10.9 0.0 copy-done.3
  10.9 65.7 %shard_map.146 = (f32[16,896,128]{2,1,0:T(8,128)}, f32[16,384]{1,0:T(8,128)}) custom-call(s32[16]{0:T(128)} %copy-done.3, bf16[16,896,128]{2,1,0:T(8,128)(2,1)} %start_ref.1, bf16[16,896,128]{2,1,0:T(8,128)(2,1)} %cost_ref.1, bf16[16,896,128]{2,1,0:T(8,128)(2,1)} %price_ref.3, bf16[8,896,128]{2,1,0:T(8,128)(2,1)} %anchor_ref.1, ...), custom_call_target="tpu_custom_call" | custom-call | tf_op jit(solution)/shard_map/pallas_call | solution.py:216
  76.6 0.0 copy-done.4
  76.6 63.2 %shard_map.147 = (bf16[16,896,128]{2,1,0:T(8,128)(2,1)}, bf16[16,896,128]{2,1,0:T(8,128)(2,1)}, bf16[1,896,128]{2,1,0:T(8,128)(2,1)}, f32[8,128]{1,0:T(8,128)}) custom-call(s32[16]{0:T(128)} %copy-done.3, f32[8,16]{1,0:T(8,128)} %fusion.pick_ref, f32[16]{0:T(128)} %copy-done.4, f32[8]{0:T(128)} %select_reduce_fusion.every_ref, f32[1]{0:T(128)} %bitcast.2.scale_ref, ...), custom_call_target="tpu_custom_call" | custom-call | tf_op jit(solution)/shard_map/pallas_call | solution.py:491
  139.9 1.2 slice.7
  141.1 0.0 copy-start
  141.1 4.4 %copy.22 = bf16[16,896,128]{2,1,0:T(8,128)(2,1)} copy(bf16[16,896,128]{2,1,0:T(8,128)(2,1)} %get-tuple-element.22) | data formatting | bytes 7340032
  145.5 0.0 copy-done
  145.5 0.0 copy-start.1
  145.5 0.0 copy-start.2
  145.5 1.8 %copy.23 = bf16[16,896,128]{2,1,0:T(8,128)(2,1)} copy(bf16[16,896,128]{2,1,0:T(8,128)(2,1)S(1)} %copy-done) | data formatting | bytes 7340032
  147.3 0.0 copy-done.1
  147.3 0.7 copy.24
  148.0 0.0 copy-done.2
  148.0 0.6 copy.25
Async XLA Ops:
  3.3 7.7 %copy-start.3 = (s32[16]{0:T(128)}, s32[16]{0:T(128)S(1)}, u32[]{:S(2)}) copy-start(s32[16]{0:T(128)S(1)} %dynamic-slice_bitcast_fusion.bundle_ref) | copy-start | bytes 196
  4.0 72.6 %copy-start.4 = (f32[16]{0:T(128)}, f32[16]{0:T(128)S(1)}, u32[]{:S(2)}) copy-start(f32[16]{0:T(128)S(1)} %dynamic-slice_convert_fusion.weight_ref) | copy-start | bytes 196
  141.1 4.4 %copy-start = (bf16[16,896,128]{2,1,0:T(8,128)(2,1)S(1)}, bf16[16,896,128]{2,1,0:T(8,128)(2,1)}, u32[]{:S(2)}) copy-start(bf16[16,896,128]{2,1,0:T(8,128)(2,1)} %get-tuple-element.23) | copy-start | bytes 11010052
  145.5 1.8 %copy-start.1 = (bf16[1,896,128]{2,1,0:T(8,128)(2,1)S(1)}, bf16[1,896,128]{2,1,0:T(8,128)(2,1)}, u32[]{:S(2)}) copy-start(bf16[1,896,128]{2,1,0:T(8,128)(2,1)} %get-tuple-element.24) | copy-start | bytes 688132
  145.5 2.5 %copy-start.2 = (f32[16,384]{1,0:T(8,128)S(1)}, f32[16,384]{1,0:T(8,128)}, u32[]{:S(2)}) copy-start(f32[16,384]{1,0:T(8,128)} %get-tuple-element.15) | copy-start | bytes 73732
